TPU v7x, 128 devices: a whole 4x4x4 slice. The times are simulated.
128 devices in a mesh: row: 8 (over x, y_hi), col: 16 (over z, y_lo, core).
Axes of the slice: x: 4, y: 4 (y_hi: 2, y_lo: 2; y = y_hi * 2 + y_lo), z: 4, core: 2. Of those that a mesh axis runs over, the one named last changes fastest.
Arguments:
- normal_slab: float32 [8192, 16384], P('row', 'col'), may hold values from -6 to 6
- left_design: float32 [3, 1024, 8192], P(None, 'col', 'row'), may hold values from -1.2 to 1.2
- right_design: float32 [3, 1024, 16384], P(None, 'row', 'col'), may hold values from -1.2 to 1.2
- estimate: float32 [16384], P('col'), may hold values from -0.25 to 0.25
- observed: float32 [3, 1024], P(None, 'row'), may hold values from -6 to 6
- arc_id: int32 [3, 1024], P(None, 'row'), may hold values from 0 to 63
- arc_bias: float32 [64], replicated, may hold values from -5 to 5
Outputs:
- updated_slab: float32 [8192, 16384], P('row', 'col')
All inputs are finite; a program needn't handle non-finite values.
Results may differ from a plain program's by a relative error of at most 0.0001.
Values sent between devices are 32-bit elements; how exact they have to be, the bound alone decides.
A program may use at most 128 MiB of HBM per device.

v0:
```python
import jax
import jax.numpy as jnp
from jax import lax
from jax.sharding import PartitionSpec as P


def gathered_total(x, axis):
    tiles = lax.all_gather(x, axis)
    return tiles.sum(axis=0)


def contract(left_rows, right_rows, weights):
    return lax.dot_general(
        left_rows * weights[:, None],
        right_rows,
        (((0,), (0,)), ((), ())),
        precision=lax.Precision.HIGHEST,
    )


def local(normal_slab, left_design, right_design, estimate, observed, arc_id, arc_bias):
    highest = lax.Precision.HIGHEST
    one_hot = arc_id[:, :, None] == jnp.arange(arc_bias.shape[0], dtype=jnp.int32)[None, None, :]
    arc_offset = jnp.sum(jnp.where(one_hot, arc_bias[None, None, :], jnp.float32(0.0)), axis=2)
    running = normal_slab
    for number in range(right_design.shape[0]):
        partial_sum = jnp.dot(right_design[number], estimate, precision=highest)
        summed = gathered_total(partial_sum, "col")
        residual = observed[number] - summed - arc_offset[number]
        weights = 1.0 / (1.0 + residual * residual)
        left_all = lax.all_gather(left_design[number], "col", axis=0, tiled=True)
        right_rows = lax.all_gather(right_design[number], "row", axis=0, tiled=True)
        weight_rows = lax.all_gather(weights, "row", axis=0, tiled=True)
        running = running + contract(left_all, right_rows, weight_rows)
    return running


def solution(mesh):
    in_specs = (
        P("row", "col"),
        P(None, "col", "row"),
        P(None, "row", "col"),
        P("col"),
        P(None, "row"),
        P(None, "row"),
        P(),
    )
    out_specs = P("row", "col")
    return jax.shard_map(local, mesh=mesh, in_specs=in_specs, out_specs=out_specs, check_vma=False)
```

profile of v0, /device:TPU:0, one launch (start us, length us, event | category | flops | bytes accessed | tf_op | source)
XLA Modules:
  0.0 381.6 jit_solution(7969491137729842434)
XLA Ops:
  6.5 0.0 copy-start
  6.5 0.0 copy-start.1
  6.5 0.0 copy-start.2
  6.5 0.0 copy-start.3
  6.5 0.0 copy-start.5
  6.5 0.0 copy-start.4
  6.6 0.0 all-gather.32.cloned.1.call-start
  6.6 2.7 fusion.23
  9.3 0.0 all-gather.32.cloned.1.call-update
  9.4 0.0 all-gather.30.cloned.1.call-start
  9.4 0.0 copy-done.2
  9.4 0.9 fusion.24
  10.4 0.0 all-gather.30.cloned.1.call-update
  10.4 0.0 all-gather.28.cloned.1.call-start
  10.4 0.7 all-gather.28.cloned.1.call-update
  11.1 0.0 all-gather.26.cloned.1.call-start
  11.2 0.5 all-gather.26.cloned.1.call-update
  11.7 0.0 all-gather.24.cloned.1.call-start
  11.7 0.5 all-gather.24.cloned.1.call-update
  12.3 0.0 all-gather.22.cloned.1.call-start
  12.3 0.5 all-gather.22.cloned.1.call-update
  12.9 0.0 copy-done
  12.9 0.0 copy-done.1
  12.9 0.5 convolution_bitcast_fusion.2
  13.4 20.9 %all-gather.9 = f32[16,1,128]{2,1,0:T(1,128)S(1)} all-gather(f32[1,1,128]{2,1,0:T(1,128)S(1)} %convolution_bitcast_fusion.2), channel_id=3, replica_groups=mesh['row'=8,'col'=16] {'col'}, dimensions={0}, use_global_device_ids=true | all-gather | bytes 8704 | tf_op jit(solution)/shard_map/all_gather | solution.py:8
  34.4 0.5 convolution_bitcast_fusion.1
  34.9 16.1 %all-gather.11 = f32[16,1,128]{2,1,0:T(1,128)S(1)} all-gather(f32[1,1,128]{2,1,0:T(1,128)S(1)} %convolution_bitcast_fusion.1), channel_id=6, replica_groups=mesh['row'=8,'col'=16] {'col'}, dimensions={0}, use_global_device_ids=true | all-gather | bytes 8704 | tf_op jit(solution)/shard_map/all_gather | solution.py:8
  51.0 0.5 convolution_bitcast_fusion
  51.5 17.6 %all-gather.13 = f32[16,1,128]{2,1,0:T(1,128)S(1)} all-gather(f32[1,1,128]{2,1,0:T(1,128)S(1)} %convolution_bitcast_fusion), channel_id=9, replica_groups=mesh['row'=8,'col'=16] {'col'}, dimensions={0}, use_global_device_ids=true | all-gather | bytes 8704 | tf_op jit(solution)/shard_map/all_gather | solution.py:8
  69.1 0.0 copy-done.3
  69.1 0.0 copy-done.5
  69.1 0.1 select_reduce_fusion
  69.2 0.0 copy-done.4
  69.3 23.1 %all-gather.14 = f32[8,1,128]{2,1,0:T(1,128)S(1)} all-gather(f32[1,1,128]{2,1,0:T(1,128)S(1)} %get-tuple-element.12), channel_id=1, replica_groups=mesh['row'=8,'col'=16] {'row'}, dimensions={0}, use_global_device_ids=true | all-gather | bytes 4608 | tf_op jit(solution)/shard_map/all_gather | solution.py:33
  92.4 18.0 %all-gather.12 = f32[8,1,128]{2,1,0:T(1,128)S(1)} all-gather(f32[1,1,128]{2,1,0:T(1,128)S(1)} %get-tuple-element.13), channel_id=1, replica_groups=mesh['row'=8,'col'=16] {'row'}, dimensions={0}, use_global_device_ids=true | all-gather | bytes 4608 | tf_op jit(solution)/shard_map/all_gather | solution.py:33
  110.3 21.5 %all-gather.10 = f32[8,1,128]{2,1,0:T(1,128)S(1)} all-gather(f32[1,1,128]{2,1,0:T(1,128)S(1)} %get-tuple-element.11), channel_id=1, replica_groups=mesh['row'=8,'col'=16] {'row'}, dimensions={0}, use_global_device_ids=true | all-gather | bytes 4608 | tf_op jit(solution)/shard_map/all_gather | solution.py:33
  131.8 0.0 all-gather.32.cloned.1.call-done
  131.8 0.0 all-gather.30.cloned.1.call-done
  131.8 18.6 %fusion = f32[1024,1024]{1,0:T(8,128)} fusion(f32[1,1024,1024]{2,1,0:T(8,128)} %all-gather.32.cloned.1.call-done, f32[1,1024,1024]{2,1,0:T(8,128)} %all-gather.30.cloned.1.call-done, f32[1024]{0:T(1024)S(1)} %bitcast.105), kind=kOutput, calls=%fused_computation | convolution fusion | flops 12885950464 | bytes 12587008 | tf_op jit(solution)/shard_map/dot_general | solution.py:13
  150.4 44.4 %all-gather.28.cloned.1.call-done = f32[1,1024,1024]{2,1,0:T(8,128)} async-done(((f32[1,128,1024]{2,1,0:T(8,128)}), f32[1,1024,1024]{2,1,0:T(8,128)}) %all-gather.28.cloned.1.call-update) | async-done | bytes 4194320 | tf_op jit(solution)/shard_map/all_gather | solution.py:32
  194.8 37.0 %all-gather.26.cloned.1.call-done = f32[1,1024,1024]{2,1,0:T(8,128)} async-done(((f32[1,64,1024]{2,1,0:T(8,128)}), f32[1,1024,1024]{2,1,0:T(8,128)}) %all-gather.26.cloned.1.call-update) | async-done | bytes 4194320 | tf_op jit(solution)/shard_map/all_gather | solution.py:31
  231.8 18.3 %fusion.2 = f32[1024,1024]{1,0:T(8,128)} fusion(f32[1,1024,1024]{2,1,0:T(8,128)} %all-gather.28.cloned.1.call-done, f32[1,1024,1024]{2,1,0:T(8,128)} %all-gather.26.cloned.1.call-done, f32[1024]{0:T(1024)S(1)} %bitcast.104), kind=kOutput, calls=%fused_computation.3 | convolution fusion | flops 12885950464 | bytes 12587008 | tf_op jit(solution)/shard_map/dot_general | solution.py:13
  250.1 55.4 %all-gather.24.cloned.1.call-done = f32[1,1024,1024]{2,1,0:T(8,128)} async-done(((f32[1,128,1024]{2,1,0:T(8,128)}), f32[1,1024,1024]{2,1,0:T(8,128)}) %all-gather.24.cloned.1.call-update) | async-done | bytes 4194320 | tf_op jit(solution)/shard_map/all_gather | solution.py:32
  305.5 37.0 %all-gather.22.cloned.1.call-done = f32[1,1024,1024]{2,1,0:T(8,128)} async-done(((f32[1,64,1024]{2,1,0:T(8,128)}), f32[1,1024,1024]{2,1,0:T(8,128)}) %all-gather.22.cloned.1.call-update) | async-done | bytes 4194320 | tf_op jit(solution)/shard_map/all_gather | solution.py:31
  342.5 32.2 %add_add_fusion = f32[1024,1024]{1,0:T(8,128)} fusion(f32[1024,1024]{1,0:T(8,128)} %fusion, f32[1024,1024]{1,0:T(8,128)} %fusion.2, f32[1024,1024]{1,0:T(8,128)} %param.7, f32[1,1024,1024]{2,1,0:T(8,128)} %all-gather.24.cloned.1.call-done, f32[1,1024,1024]{2,1,0:T(8,128)} %all-gather.22.cloned.1.call-done, f32[1024]{0:T(1024)S(1)} %bitcast.103), kind=kOutput, calls=%fused_computation.9 | convolution fusion | flops 12889096192 | bytes 25169920 | tf_op jit(solution)/shard_map/dot_general | solution.py:13
  (4 shorter events, 0.1 us)
Async XLA Ops:
  6.5 6.3 %copy-start = (f32[1024]{0:T(1024)S(1)}, f32[1024]{0:T(1024)}, u32[]{:S(2)}) copy-start(f32[1024]{0:T(1024)} %param.10) | copy-start | bytes 12292
  6.5 6.3 %copy-start.1 = (f32[3,128,1024]{2,1,0:T(8,128)S(1)}, f32[3,128,1024]{2,1,0:T(8,128)}, u32[]{:S(2)}) copy-start(f32[3,128,1024]{2,1,0:T(8,128)} %param.9) | copy-start | bytes 4718596
  6.5 2.9 copy-start.2
  6.5 62.6 %copy-start.3 = (s32[3,128]{1,0:T(4,128)S(1)}, s32[3,128]{1,0:T(4,128)}, u32[]{:S(2)}) copy-start(s32[3,128]{1,0:T(4,128)} %param.12) | copy-start | bytes 4612
  6.5 62.6 %copy-start.5 = (f32[64]{0:T(128)S(1)}, f32[64]{0:T(128)}, u32[]{:S(2)}) copy-start(f32[64]{0:T(128)} %param.13) | copy-start | bytes 772
  6.5 62.7 %copy-start.4 = (f32[3,128]{1,0:T(4,128)S(1)}, f32[3,128]{1,0:T(4,128)}, u32[]{:S(2)}) copy-start(f32[3,128]{1,0:T(4,128)} %param.11) | copy-start | bytes 4612
  6.6 125.3 %all-gather.32.cloned.1.call-start = ((), (), s32[]{:S(2)}) async-start(), calls=%async_computation.5 | async-start | bytes 4718592 | tf_op jit(solution)/shard_map/all_gather | solution.py:32
  9.4 122.5 %all-gather.30.cloned.1.call-start = ((), (), s32[]{:S(2)}) async-start(), calls=%async_computation.4 | async-start | bytes 4456448 | tf_op jit(solution)/shard_map/all_gather | solution.py:31
  10.4 184.4 %all-gather.28.cloned.1.call-start = ((), (), s32[]{:S(2)}) async-start(), calls=%async_computation.3 | async-start | bytes 4718592 | tf_op jit(solution)/shard_map/all_gather | solution.py:32
  11.1 220.7 %all-gather.26.cloned.1.call-start = ((), (), s32[]{:S(2)}) async-start(), calls=%async_computation.2 | async-start | bytes 4456448 | tf_op jit(solution)/shard_map/all_gather | solution.py:31
  11.7 293.8 %all-gather.24.cloned.1.call-start = ((), (), s32[]{:S(2)}) async-start(), calls=%async_computation.1 | async-start | bytes 4718592 | tf_op jit(solution)/shard_map/all_gather | solution.py:32
  12.3 330.2 %all-gather.22.cloned.1.call-start = ((), (), s32[]{:S(2)}) async-start(), calls=%async_computation | async-start | bytes 4456448 | tf_op jit(solution)/shard_map/all_gather | solution.py:31
Sparse Core Ops, SparseCore 0:
  9.7 74.0 all-gather.31
  85.5 35.4 all-gather.29
  123.4 71.3 all-gather.27
  196.4 35.3 all-gather.25
  234.0 71.4 all-gather.23
  307.1 35.3 all-gather.21
where the time goes:
time: 383 us; the launch traced here: 382 us
  waiting for transfers between devices  176 us (46%)
  blocking collectives  117 us (31%)
  matrix products  70.6 us (18%)
  between operations  13.5 us (4%)
    all_gather x3, waiting for transfers between devices, local(): right_rows = lax.all_gather(right_design[number], 'row', axis=0, tiled=True)  99.8 us
    all_gather x3, waiting for transfers between devices, local(): left_all = lax.all_gather(left_design[number], 'col', axis=0, tiled=True)  73.9 us
    dot_general x3, matrix products, contract(): lax.dot_general(left_rows * weights[:, None], right_rows, (((0,), (0,)),...  69.1 us
    all_gather x3, blocking collectives, local(): weight_rows = lax.all_gather(weights, 'row', axis=0, tiled=True)  62.6 us
    all_gather x3, blocking collectives, gathered_total(): tiles = lax.all_gather(x, axis)  54.6 us
  transfers between devices with their start and end apart: 6, of which 4 were waited for; matrix products, arithmetic and copies ran while one was open for 10% of the time, Pallas kernels for 0%

commit v1 on v0

v1 whole, which is shorter than its diff:
```python
import functools

import jax
import jax.numpy as jnp
from jax import lax
from jax.experimental import pallas as pl
from jax.experimental.pallas import tpu as pltpu
from jax.sharding import PartitionSpec as P

MESH = pl.DeviceIdType.MESH
F32, BF16 = jnp.float32, jnp.bfloat16
NX, NZ = 4, 4
TILE = 256


def kernel(est, obs, arc, bias, slab, left, right, out, rbuf, lbuf, lt, psend, pbuf, wbuf,
           rs, rr, ls, lr, ps, pr, ws, wr, cs):
    groups, n_obs, width = right.shape
    half, quarter = n_obs // 2, n_obs // 4
    row, col = lax.axis_index("row"), lax.axis_index("col")
    x, h = row // 2, row % 2
    z, l, k = col // 4, (col // 2) % 2, col % 2

    def unit_r(dx, flip=0):
        return ((x + dx) % NX) * 2 + (h + flip) % 2

    def unit_l(dz, flip=0):
        return ((z + dz) % NZ) * 2 + (l + flip) % 2

    def to_row(r):
        return (r, col)

    def to_col(c):
        return (row, c)

    x_up, x_down, y_far = to_row(unit_r(1)), to_row(unit_r(-1)), to_row(unit_r(0, 1))
    z_up, z_down = to_col(unit_l(1) * 2 + k), to_col(unit_l(-1) * 2 + k)
    y_near, sibling = to_col(unit_l(0, 1) * 2 + k), to_col((col // 2) * 2 + (1 - k))

    barrier = pltpu.get_barrier_semaphore()
    for d in range(1, 16):
        pl.semaphore_signal(barrier, inc=1, device_id=to_col((col + d) % 16), device_id_type=MESH)
    for d in range(1, 8):
        pl.semaphore_signal(barrier, inc=1, device_id=to_row((row + d) % 8), device_id_type=MESH)
    pl.semaphore_wait(barrier, 22)

    sends = []

    def remote(src, dst, s, r, target):
        return pltpu.make_async_remote_copy(
            src_ref=src, dst_ref=dst, send_sem=s, recv_sem=r, device_id=target, device_id_type=MESH
        )

    A, B = pl.ds(0, half), pl.ds(half, half)

    def r_copy(slot, unit, part, target, src=None):
        dst = rbuf.at[unit, :, part, :]
        return remote(dst if src is None else src.at[:, part, :], dst, rs.at[slot], rr.at[slot], target)

    def r_send(slot, unit, part, target, src=None):
        c = r_copy(slot, unit, part, target, src)
        c.start()
        sends.append(c)

    def r_wait(slot, unit, part):
        r_copy(slot, unit, part, y_far).wait_recv()

    def l_rows(part, core):
        if part == "a":
            return pl.ds(core * half, quarter)
        if part == "b":
            return pl.ds(core * half + quarter, quarter)
        return pl.ds(core * half, half)

    def l_copy(slot, unit, part, target, src=None, core=None):
        dst = lbuf.at[unit, :, l_rows(part, k if core is None else core), :]
        if src is not None:
            src = src.at[:, l_rows(part, 0), :]
        return remote(dst if src is None else src, dst, ls.at[slot], lr.at[slot], target)

    def l_send(slot, unit, part, target, src=None):
        c = l_copy(slot, unit, part, target, src)
        c.start()
        sends.append(c)

    def l_wait(slot, unit, part, core=None):
        l_copy(slot, unit, part, sibling, core=core).wait_recv()

    own_r, own_l = row, col // 2
    l_send(0, own_l, "", y_near, left)
    l_send(1, own_l, "a", z_up, left)
    l_send(4, own_l, "b", z_down, left)
    l_send(2, own_l, "b", z_up, left)
    l_send(3, own_l, "a", z_down, left)
    r_send(0, own_r, A, x_up, right)
    r_send(3, own_r, B, x_down, right)
    r_send(4, own_r, A, y_far, right)
    r_send(1, own_r, B, x_up, right)
    r_send(2, own_r, A, x_down, right)
    r_send(5, own_r, B, y_far, right)
    l_send(13, own_l, "", sibling, left)
    r_here = pltpu.make_async_copy(right, rbuf.at[own_r], cs.at[0])
    l_here = pltpu.make_async_copy(left, lbuf.at[own_l, :, l_rows("", k), :], cs.at[1])
    s_here = pltpu.make_async_copy(slab, out, cs.at[2])
    r_here.start()
    l_here.start()
    s_here.start()

    r_here.wait()
    e = jnp.broadcast_to(est[...], (8, width))
    psend[...] = jnp.zeros_like(psend)
    for g in range(groups):
        p = lax.dot_general(
            e, rbuf[own_r, g], (((1,), (1,)), ((), ())),
            precision=lax.Precision.HIGHEST, preferred_element_type=F32,
        )
        psend[g : g + 1, :] = p[0:1, :]
    for d in range(1, 16):
        c = remote(psend, pbuf.at[col], ps.at[d], pr.at[d], to_col((col + d) % 16))
        c.start()
        sends.append(c)
    offset = jnp.zeros((groups, n_obs), F32)
    ids = arc[...]
    for a in range(bias.shape[0]):
        offset = jnp.where(ids == a, bias[a], offset)
    pbuf[col] = psend[...]
    for d in range(1, 16):
        remote(psend, pbuf.at[(col + 16 - d) % 16], ps.at[d], pr.at[d], sibling).wait_recv()
    total = pbuf[0]
    for c in range(1, 16):
        total = total + pbuf[c]
    residual = obs[...] - total[:groups] - offset
    wbuf[row] = jnp.zeros_like(wbuf[0])
    wbuf[row, 0:groups, :] = 1.0 / (1.0 + residual * residual)
    for d in range(1, 8):
        c = remote(wbuf.at[row], wbuf.at[row], ws.at[d], wr.at[d], to_row((row + d) % 8))
        c.start()
        sends.append(c)

    def prepare(unit):
        def body(i, carry):
            cols = pl.ds(pl.multiple_of(i * TILE, TILE), TILE)
            for g in range(groups):
                t = lbuf[unit, g, :, cols].T * wbuf[unit, g : g + 1, :]
                hi = t.astype(BF16)
                lo = (t - hi.astype(F32)).astype(BF16)
                lt[unit, cols, g * n_obs : (g + 1) * n_obs] = hi
                lt[unit, cols, (groups + g) * n_obs : (groups + g + 1) * n_obs] = lo
            return carry

        lax.fori_loop(0, width // TILE, body, 0)

    depth = groups * n_obs

    def multiply(unit):
        def body(i, carry):
            cols = pl.ds(pl.multiple_of(i * TILE, TILE), TILE)
            t = rbuf[unit, :, :, cols].reshape(depth, TILE)
            hi = t.astype(BF16)
            lo = (t - hi.astype(F32)).astype(BF16)
            both = jnp.concatenate([hi, hi], axis=0)
            out[:, cols] += jnp.dot(lt[unit], both, preferred_element_type=F32) + jnp.dot(
                lt[unit, :, 0:depth], lo, preferred_element_type=F32
            )
            return carry

        lax.fori_loop(0, width // TILE, body, 0)

    l_wait(1, unit_l(-1), "a")
    l_send(5, unit_l(-1), "a", z_up)
    l_wait(4, unit_l(1), "b")
    l_send(6, unit_l(1), "b", z_down)
    l_wait(0, unit_l(0, 1), "")
    l_send(7, unit_l(0, 1), "a", z_up)
    l_send(10, unit_l(0, 1), "b", z_down)
    l_send(8, unit_l(0, 1), "b", z_up)
    l_send(9, unit_l(0, 1), "a", z_down)
    l_send(14, unit_l(0, 1), "", sibling)
    l_wait(2, unit_l(-1), "b")
    l_send(15, unit_l(-1), "", sibling)
    l_wait(3, unit_l(1), "a")
    l_send(16, unit_l(1), "", sibling)
    for d in range(1, 8):
        u = (row + 8 - d) % 8
        remote(wbuf.at[row], wbuf.at[u], ws.at[d], wr.at[d], y_far).wait_recv()
    l_here.wait()
    l_wait(13, own_l, "", 1 - k)
    prepare(own_l)
    r_wait(0, unit_r(-1), A)
    r_send(6, unit_r(-1), A, x_up)
    r_send(8, unit_r(-1), A, y_far)
    r_wait(3, unit_r(1), B)
    r_send(7, unit_r(1), B, x_down)
    r_send(9, unit_r(1), B, y_far)
    l_wait(5, unit_l(2), "a")
    l_wait(6, unit_l(2), "b")
    l_send(17, unit_l(2), "", sibling)
    r_wait(4, unit_r(0, 1), A)
    r_send(10, unit_r(0, 1), A, x_down)
    r_wait(5, unit_r(0, 1), B)
    r_send(11, unit_r(0, 1), B, x_up)
    l_wait(14, unit_l(0, 1), "", 1 - k)
    prepare(unit_l(0, 1))
    l_wait(15, unit_l(-1), "", 1 - k)
    prepare(unit_l(-1))
    l_wait(7, unit_l(-1, 1), "a")
    l_send(11, unit_l(-1, 1), "a", z_up)
    l_wait(10, unit_l(1, 1), "b")
    l_send(12, unit_l(1, 1), "b", z_down)
    l_wait(16, unit_l(1), "", 1 - k)
    prepare(unit_l(1))
    l_wait(8, unit_l(-1, 1), "b")
    l_send(18, unit_l(-1, 1), "", sibling)
    l_wait(9, unit_l(1, 1), "a")
    l_send(19, unit_l(1, 1), "", sibling)
    l_wait(17, unit_l(2), "", 1 - k)
    prepare(unit_l(2))
    l_wait(18, unit_l(-1, 1), "", 1 - k)
    prepare(unit_l(-1, 1))
    l_wait(19, unit_l(1, 1), "", 1 - k)
    prepare(unit_l(1, 1))
    r_wait(1, unit_r(-1), B)
    r_wait(2, unit_r(1), A)
    l_wait(11, unit_l(2, 1), "a")
    l_wait(12, unit_l(2, 1), "b")
    l_send(20, unit_l(2, 1), "", sibling)
    r_wait(8, unit_r(-1, 1), A)
    r_send(12, unit_r(-1, 1), A, x_up)
    r_wait(9, unit_r(1, 1), B)
    r_send(13, unit_r(1, 1), B, x_down)
    l_wait(20, unit_l(2, 1), "", 1 - k)
    prepare(unit_l(2, 1))
    s_here.wait()
    multiply(own_r)
    multiply(unit_r(-1))
    multiply(unit_r(1))
    multiply(unit_r(0, 1))
    r_wait(6, unit_r(2), A)
    r_wait(7, unit_r(2), B)
    multiply(unit_r(2))
    r_wait(10, unit_r(1, 1), A)
    multiply(unit_r(1, 1))
    r_wait(11, unit_r(-1, 1), B)
    multiply(unit_r(-1, 1))
    r_wait(12, unit_r(2, 1), A)
    r_wait(13, unit_r(2, 1), B)
    multiply(unit_r(2, 1))
    for c in sends:
        c.wait_send()


def local(normal_slab, left_design, right_design, estimate, observed, arc_id, arc_bias):
    groups, n_obs, width = right_design.shape
    rows = left_design.shape[2]
    vmem, smem, anyspace = (
        pl.BlockSpec(memory_space=m) for m in (pltpu.VMEM, pltpu.SMEM, pl.ANY)
    )
    dma = pltpu.SemaphoreType.DMA
    return pl.pallas_call(
        kernel,
        name="gather_and_update",
        out_shape=jax.ShapeDtypeStruct(normal_slab.shape, F32),
        in_specs=[vmem, vmem, vmem, smem, anyspace, anyspace, anyspace],
        out_specs=vmem,
        scratch_shapes=[
            pltpu.VMEM((8, groups, n_obs, width), F32),
            pltpu.VMEM((8, groups, n_obs, rows), F32),
            pltpu.VMEM((8, rows, 2 * groups * n_obs), BF16),
            pltpu.VMEM((8, n_obs), F32),
            pltpu.VMEM((16, 8, n_obs), F32),
            pltpu.VMEM((8, 8, n_obs), F32),
            dma((14,)), dma((14,)), dma((21,)), dma((21,)),
            dma((16,)), dma((16,)), dma((8,)), dma((8,)), dma((3,)),
        ],
        compiler_params=pltpu.CompilerParams(
            collective_id=0, has_side_effects=True, vmem_limit_bytes=60 * 1024 * 1024
        ),
    )(estimate[None, :], observed, arc_id, arc_bias, normal_slab, left_design, right_design)


def solution(mesh):
    in_specs = (
        P("row", "col"),
        P(None, "col", "row"),
        P(None, "row", "col"),
        P("col"),
        P(None, "row"),
        P(None, "row"),
        P(),
    )
    return jax.shard_map(local, mesh=mesh, in_specs=in_specs, out_specs=P("row", "col"), check_vma=False)
```

time: 383 us -> 139 us (0.36)
  waiting for transfers between devices: 176 us -> 0 us
  Pallas kernels: 0 us -> 134 us
  blocking collectives: 117 us -> 0 us
  matrix products: 70.6 us -> 0 us
  between operations: 13.5 us -> 0.01 us
    all_gather x6 -> x0, waiting for transfers between devices: 174 us -> none  [the longest x3 99.8 us: local(): right_rows = lax.all_gather(right_design[number], 'row', axis=0, tiled=True)]
    pallas_call x0 -> x1, Pallas kernels: none -> 134 us  [local(): pl.pallas_call(kernel, name='gather_and_update', out_shape=jax.ShapeDtype...]
    all_gather x6 -> x0, blocking collectives: 117 us -> none  [the longest x3 62.6 us: local(): weight_rows = lax.all_gather(weights, 'row', axis=0, tiled=True)]
    dot_general x6 -> x0, matrix products: 70.6 us -> none  [the longest x3 69.1 us: contract(): lax.dot_general(left_rows * weights[:, None], right_rows, (((0,), (0,)),...]
    unnamed x12 -> x1, local copies, waits for them, and re-layouts: 0.02 us -> 4.79 us
  transfers between devices with their start and end apart: 6 -> 0, of which waited for: 4 -> 0; matrix products, arithmetic and copies ran while one was open for 10% -> 0% of each run, Pallas kernels for 0% -> 0%
where the time goes in v1:
time: 139 us
  Pallas kernels  134 us (96%)
  local copies, waits for them, and re-layouts  4.79 us (3%)
    pallas_call x1, Pallas kernels, local(): pl.pallas_call(kernel, name='gather_and_update', out_shape=jax.ShapeDtype...  134 us
    unnamed x1, local copies, waits for them, and re-layouts  4.79 us

profile of v1, /device:TPU:0, one launch (start us, length us, event | category | flops | bytes accessed | tf_op | source)
XLA Modules:
  0.0 139.0 jit_solution(5920878541376058431)
XLA Ops:
  0.0 134.2 %gather_and_update.1 = f32[1024,1024]{1,0:T(8,128)} custom-call(f32[1,1024]{1,0:T(1,128)} %bitcast.1, f32[3,128]{1,0:T(4,128)} %obs.1, s32[3,128]{1,0:T(4,128)} %arc.1, f32[64]{0:T(128)} %bias.1, f32[1024,1024]{1,0:T(8,128)} %slab.1, f32[3,64,1024]{2,1,0:T(8,128)} %left.1, f32[3,128,1024]{2,1,0:T(8,128)} %right.1), custom_call_target="tpu_custom_call" | custom-call | tf_op jit(solution)/shard_map/gather_and_update/pallas_call | solution.py:259
  134.2 4.8 %copy.9 = f32[1024,1024]{1,0:T(8,128)} copy(f32[1024,1024]{1,0:T(8,128)} %gather_and_update.1) | data formatting | bytes 8388608

commit v2 on v1

v2 whole, which is shorter than its diff:
```python
import functools

import jax
import jax.numpy as jnp
from jax import lax
from jax.experimental import pallas as pl
from jax.experimental.pallas import tpu as pltpu
from jax.sharding import PartitionSpec as P

MESH = pl.DeviceIdType.MESH
F32, BF16 = jnp.float32, jnp.bfloat16
NX, NZ = 4, 4
PIECES = 4
ALONG_X = (3,)
A, B = 0, 1
TILE = 256


def kernel(est_in, obs_in, arc_in, bias_in, slab, left, right, out, rbuf, lbuf, lt, psend, pbuf, wbuf,
           est, obs, arc, bias, rs, rr, ls, lr, ps, pr, ws, wr, cs):
    groups, n_obs, width = right.shape
    half, quarter = n_obs // 2, n_obs // 4
    row, col = lax.axis_index("row"), lax.axis_index("col")
    x, h = row // 2, row % 2
    z, l, k = col // 4, (col // 2) % 2, col % 2

    def unit_r(dx, flip=0):
        return ((x + dx) % NX) * 2 + (h + flip) % 2

    def unit_l(dz, flip=0):
        return ((z + dz) % NZ) * 2 + (l + flip) % 2

    def to_row(r):
        return (r, col)

    def to_col(c):
        return (row, c)

    x_up, x_down, y_far = to_row(unit_r(1)), to_row(unit_r(-1)), to_row(unit_r(0, 1))
    z_up, z_down = to_col(unit_l(1) * 2 + k), to_col(unit_l(-1) * 2 + k)
    y_near, sibling = to_col(unit_l(0, 1) * 2 + k), to_col((col // 2) * 2 + (1 - k))

    r_here = pltpu.make_async_copy(right, rbuf.at[row], cs.at[0])
    l_here = pltpu.make_async_copy(left, lbuf.at[col // 2, :, pl.ds(k * half, half), :], cs.at[1])
    s_here = pltpu.make_async_copy(slab, out, cs.at[2])
    small = [
        pltpu.make_async_copy(src, dst, cs.at[3 + i])
        for i, (src, dst) in enumerate([(est_in, est), (obs_in, obs), (arc_in, arc), (bias_in, bias)])
    ]
    for c in [r_here, *small, l_here, s_here]:
        c.start()

    barrier = pltpu.get_barrier_semaphore()
    for d in range(1, 16):
        pl.semaphore_signal(barrier, inc=1, device_id=to_col((col + d) % 16), device_id_type=MESH)
    for d in range(1, 8):
        pl.semaphore_signal(barrier, inc=1, device_id=to_row((row + d) % 8), device_id_type=MESH)
    pl.semaphore_wait(barrier, 22)

    sends = []

    def remote(src, dst, s, r, target):
        return pltpu.make_async_remote_copy(
            src_ref=src, dst_ref=dst, send_sem=s, recv_sem=r, device_id=target, device_id_type=MESH
        )

    def r_copy(slot, unit, part, i, target, src=None):
        rows, cols = pl.ds(part * half, half), pl.ds(i * TILE, TILE)
        dst = rbuf.at[unit, :, rows, cols]
        s = slot * PIECES + i
        return remote(dst if src is None else src.at[:, rows, cols], dst, rs.at[s], rr.at[s], target)

    def r_send(slot, unit, part, i, target, src=None):
        c = r_copy(slot, unit, part, i, target, src)
        c.start()
        sends.append(c)

    def r_wait(slot, unit, part, i):
        r_copy(slot, unit, part, i, y_far).wait_recv()

    def r_all(slot, unit, part):
        for i in range(PIECES):
            r_wait(slot, unit, part, i)

    def l_rows(part, core):
        if part == "a":
            return pl.ds(core * half, quarter)
        if part == "b":
            return pl.ds(core * half + quarter, quarter)
        return pl.ds(core * half, half)

    def l_copy(slot, unit, part, target, src=None, core=None):
        dst = lbuf.at[unit, :, l_rows(part, k if core is None else core), :]
        if src is not None:
            src = src.at[:, l_rows(part, 0), :]
        return remote(dst if src is None else src, dst, ls.at[slot], lr.at[slot], target)

    def l_send(slot, unit, part, target, src=None):
        c = l_copy(slot, unit, part, target, src)
        c.start()
        sends.append(c)
        return c

    def l_wait(slot, unit, part, core=None):
        l_copy(slot, unit, part, sibling, core=core).wait_recv()

    own_r, own_l = row, col // 2
    near = l_send(0, own_l, "", y_near, left)
    for i in range(PIECES):
        r_send(0, own_r, A, i, x_up, right)
        r_send(3, own_r, B, i, x_down, right)
    l_send(1, own_l, "a", z_up, left)
    l_send(4, own_l, "b", z_down, left)
    l_send(2, own_l, "b", z_up, left)
    l_send(3, own_l, "a", z_down, left)
    for i in range(PIECES):
        r_send(1, own_r, B, i, x_up, right)
        r_send(2, own_r, A, i, x_down, right)
    l_send(13, own_l, "", sibling, left)
    r_here.wait()
    for c in small:
        c.wait()
    e = jnp.broadcast_to(est[...], (8, width))
    psend[...] = jnp.zeros_like(psend)
    for g in range(groups):
        p = lax.dot_general(
            e, rbuf[own_r, g], (((1,), (1,)), ((), ())),
            precision=lax.Precision.HIGHEST, preferred_element_type=F32,
        )
        psend[g : g + 1, :] = p[0:1, :]
    for d in range(1, 16):
        c = remote(psend, pbuf.at[col], ps.at[d], pr.at[d], to_col((col + d) % 16))
        c.start()
        sends.append(c)
    offset = jnp.zeros((groups, n_obs), F32)
    ids = arc[...]
    for a in range(bias.shape[0]):
        offset = jnp.where(ids == a, bias[a], offset)
    pbuf[col] = psend[...]
    for d in range(1, 16):
        remote(psend, pbuf.at[(col + 16 - d) % 16], ps.at[d], pr.at[d], sibling).wait_recv()
    total = pbuf[0]
    for c in range(1, 16):
        total = total + pbuf[c]
    residual = obs[...] - total[:groups] - offset
    wbuf[row] = jnp.zeros_like(wbuf[0])
    wbuf[row, 0:groups, :] = 1.0 / (1.0 + residual * residual)
    for d in range(1, 8):
        c = remote(wbuf.at[row], wbuf.at[row], ws.at[d], wr.at[d], to_row((row + d) % 8))
        c.start()
        sends.append(c)

    def prepare(unit):
        def body(i, carry):
            cols = pl.ds(pl.multiple_of(i * TILE, TILE), TILE)
            for g in range(groups):
                t = lbuf[unit, g, :, cols].T * wbuf[unit, g : g + 1, :]
                hi = t.astype(BF16)
                lo = (t - hi.astype(F32)).astype(BF16)
                lt[unit, cols, g * n_obs : (g + 1) * n_obs] = hi
                lt[unit, cols, (groups + g) * n_obs : (groups + g + 1) * n_obs] = lo
            return carry

        lax.fori_loop(0, width // TILE, body, 0)

    depth = groups * n_obs

    def multiply_part(unit, i):
        cols = pl.ds(pl.multiple_of(i * TILE, TILE), TILE)
        t = rbuf[unit, :, :, cols].reshape(depth, TILE)
        hi = t.astype(BF16)
        lo = (t - hi.astype(F32)).astype(BF16)
        both = jnp.concatenate([hi, hi], axis=0)
        out[:, cols] += jnp.dot(lt[unit], both, preferred_element_type=F32) + jnp.dot(
            lt[unit, :, 0:depth], lo, preferred_element_type=F32
        )

    def multiply(*units):
        def body(i, carry):
            for unit in units:
                multiply_part(unit, i)
            return carry

        lax.fori_loop(0, PIECES, body, 0)

    def first(i):
        r_wait(0, unit_r(-1), A, i)
        if i not in ALONG_X:
            r_send(8, unit_r(-1), A, i, y_far)
        r_send(6, unit_r(-1), A, i, x_up)
        r_wait(3, unit_r(1), B, i)
        if i not in ALONG_X:
            r_send(9, unit_r(1), B, i, y_far)
        r_send(7, unit_r(1), B, i, x_down)

    def second(i):
        r_wait(4, unit_r(0, 1), A, i)
        if i in ALONG_X:
            r_send(8, unit_r(0, 1), A, i, x_up)
        r_send(10, unit_r(0, 1), A, i, x_down)
        r_wait(5, unit_r(0, 1), B, i)
        if i in ALONG_X:
            r_send(9, unit_r(0, 1), B, i, x_down)
        r_send(11, unit_r(0, 1), B, i, x_up)

    def third(i):
        r_wait(8, unit_r(-1, 1), A, i)
        r_send(12, unit_r(-1, 1), A, i, x_up)
        r_wait(9, unit_r(1, 1), B, i)
        r_send(13, unit_r(1, 1), B, i, x_down)

    near.wait_send()
    sends.remove(near)
    for i in range(PIECES):
        r_send(4, own_r, A, i, y_far, right)
        r_send(5, own_r, B, i, y_far, right)
    l_wait(1, unit_l(-1), "a")
    l_send(5, unit_l(-1), "a", z_up)
    l_wait(4, unit_l(1), "b")
    l_send(6, unit_l(1), "b", z_down)
    for i in range(PIECES):
        first(i)
    l_wait(0, unit_l(0, 1), "")
    l_send(7, unit_l(0, 1), "a", z_up)
    l_send(10, unit_l(0, 1), "b", z_down)
    l_send(8, unit_l(0, 1), "b", z_up)
    l_send(9, unit_l(0, 1), "a", z_down)
    l_send(14, unit_l(0, 1), "", sibling)
    for d in range(1, 8):
        u = (row + 8 - d) % 8
        remote(wbuf.at[row], wbuf.at[u], ws.at[d], wr.at[d], y_far).wait_recv()
    l_here.wait()
    l_wait(13, own_l, "", 1 - k)
    prepare(own_l)
    l_wait(2, unit_l(-1), "b")
    l_send(15, unit_l(-1), "", sibling)
    l_wait(3, unit_l(1), "a")
    l_send(16, unit_l(1), "", sibling)
    l_wait(14, unit_l(0, 1), "", 1 - k)
    prepare(unit_l(0, 1))
    second(0)
    l_wait(5, unit_l(2), "a")
    l_wait(6, unit_l(2), "b")
    l_send(17, unit_l(2), "", sibling)
    l_wait(15, unit_l(-1), "", 1 - k)
    prepare(unit_l(-1))
    l_wait(7, unit_l(-1, 1), "a")
    l_send(11, unit_l(-1, 1), "a", z_up)
    l_wait(10, unit_l(1, 1), "b")
    l_send(12, unit_l(1, 1), "b", z_down)
    second(1)
    l_wait(16, unit_l(1), "", 1 - k)
    prepare(unit_l(1))
    second(2)
    l_wait(17, unit_l(2), "", 1 - k)
    prepare(unit_l(2))
    l_wait(8, unit_l(-1, 1), "b")
    l_send(18, unit_l(-1, 1), "", sibling)
    l_wait(9, unit_l(1, 1), "a")
    l_send(19, unit_l(1, 1), "", sibling)
    second(3)
    l_wait(18, unit_l(-1, 1), "", 1 - k)
    prepare(unit_l(-1, 1))
    l_wait(11, unit_l(2, 1), "a")
    l_wait(12, unit_l(2, 1), "b")
    l_send(20, unit_l(2, 1), "", sibling)
    l_wait(19, unit_l(1, 1), "", 1 - k)
    prepare(unit_l(1, 1))
    s_here.wait()
    l_wait(20, unit_l(2, 1), "", 1 - k)
    prepare(unit_l(2, 1))
    multiply(own_r)
    third(0)
    r_all(1, unit_r(-1), B)
    multiply(unit_r(-1))
    third(1)
    r_all(2, unit_r(1), A)
    multiply(unit_r(1))
    multiply(unit_r(0, 1))
    third(2)
    r_all(6, unit_r(2), A)
    r_all(7, unit_r(2), B)
    multiply(unit_r(2))
    for i in range(PIECES):
        if i == PIECES - 1:
            third(i)
        r_wait(10, unit_r(1, 1), A, i)
        multiply_part(unit_r(1, 1), i)
        r_wait(11, unit_r(-1, 1), B, i)
        multiply_part(unit_r(-1, 1), i)
    for i in range(PIECES):
        r_wait(12, unit_r(2, 1), A, i)
        r_wait(13, unit_r(2, 1), B, i)
        multiply_part(unit_r(2, 1), i)
    for c in sends:
        c.wait_send()


def local(normal_slab, left_design, right_design, estimate, observed, arc_id, arc_bias):
    groups, n_obs, width = right_design.shape
    rows = left_design.shape[2]
    dma = pltpu.SemaphoreType.DMA
    return pl.pallas_call(
        kernel,
        name="gather_and_update",
        out_shape=pltpu.VMEM(normal_slab.shape, F32),
        in_specs=[pl.BlockSpec(memory_space=pltpu.HBM)] * 7,
        out_specs=pl.BlockSpec(memory_space=pltpu.VMEM),
        scratch_shapes=[
            pltpu.VMEM((8, groups, n_obs, width), F32),
            pltpu.VMEM((8, groups, n_obs, rows), F32),
            pltpu.VMEM((8, rows, 2 * groups * n_obs), BF16),
            pltpu.VMEM((8, n_obs), F32),
            pltpu.VMEM((16, 8, n_obs), F32),
            pltpu.VMEM((8, 8, n_obs), F32),
            pltpu.VMEM((1, width), F32),
            pltpu.VMEM((groups, n_obs), F32),
            pltpu.VMEM((groups, n_obs), jnp.int32),
            pltpu.SMEM(arc_bias.shape, F32),
            dma((14 * PIECES,)), dma((14 * PIECES,)), dma((21,)), dma((21,)),
            dma((16,)), dma((16,)), dma((8,)), dma((8,)), dma((7,)),
        ],
        compiler_params=pltpu.CompilerParams(
            collective_id=0, has_side_effects=True, vmem_limit_bytes=59 * 1024 * 1024
        ),
    )(estimate[None, :], observed, arc_id, arc_bias, normal_slab, left_design, right_design)


def solution(mesh):
    in_specs = (
        P("row", "col"),
        P(None, "col", "row"),
        P(None, "row", "col"),
        P("col"),
        P(None, "row"),
        P(None, "row"),
        P(),
    )
    return jax.shard_map(local, mesh=mesh, in_specs=in_specs, out_specs=P("row", "col"), check_vma=False)
```

time: 139 us -> 116 us (0.83)
  Pallas kernels: 134 us -> 114 us
  local copies, waits for them, and re-layouts: 4.79 us -> 2.02 us
    pallas_call x1, Pallas kernels: 134 us -> 114 us  [local(): pl.pallas_call(kernel, name='gather_and_update', out_shape=pltpu.VMEM(nor...]
    unnamed x1, local copies, waits for them, and re-layouts: 4.79 us -> 2.02 us
where the time goes in v2:
time: 116 us
  Pallas kernels  114 us (98%)
  local copies, waits for them, and re-layouts  2.02 us (2%)
    pallas_call x1, Pallas kernels, local(): pl.pallas_call(kernel, name='gather_and_update', out_shape=pltpu.VMEM(nor...  114 us

profile of v2, /device:TPU:0, one launch (start us, length us, event | category | flops | bytes accessed | tf_op | source)
XLA Modules:
  0.0 115.6 jit_solution(17725045205662664842)
XLA Ops:
  0.0 113.6 %gather_and_update.1 = f32[1024,1024]{1,0:T(8,128)S(1)} custom-call(f32[1,1024]{1,0:T(1,128)} %bitcast.1, f32[3,128]{1,0:T(4,128)} %obs_in.1, s32[3,128]{1,0:T(4,128)} %arc_in.1, f32[64]{0:T(128)} %bias_in.1, f32[1024,1024]{1,0:T(8,128)} %slab.1, f32[3,64,1024]{2,1,0:T(8,128)} %left.1, f32[3,128,1024]{2,1,0:T(8,128)} %right.1), custom_call_target="tpu_custom_call" | custom-call | tf_op jit(solution)/shard_map/gather_and_update/pallas_call | solution.py:303
  113.6 2.0 %copy.9 = f32[1024,1024]{1,0:T(8,128)} copy(f32[1024,1024]{1,0:T(8,128)S(1)} %gather_and_update.1) | data formatting | bytes 8388608

commit v3 on v2

v3 whole, which is shorter than its diff:
```python
import functools

import jax
import jax.numpy as jnp
from jax import lax
from jax.experimental import pallas as pl
from jax.experimental.pallas import tpu as pltpu
from jax.sharding import PartitionSpec as P

MESH = pl.DeviceIdType.MESH
F32, BF16 = jnp.float32, jnp.bfloat16
NX, NZ = 4, 4
CHUNKS = ((0, 256), (256, 256), (512, 256), (768, 128), (896, 128))
OF_TILE = ((0,), (1,), (2,), (3, 4))
ALONG_X = (4,)
A, B = 0, 1
TILE = 256


def kernel(est_in, obs_in, arc_in, bias_in, slab, left, right, out, rbuf, lbuf, lt, psend, pbuf, wbuf,
           est, obs, arc, bias, rs, rr, ls, lr, ps, pr, ws, wr, cs):
    groups, n_obs, width = right.shape
    half, quarter = n_obs // 2, n_obs // 4
    row, col = lax.axis_index("row"), lax.axis_index("col")
    x, h = row // 2, row % 2
    z, l, k = col // 4, (col // 2) % 2, col % 2

    def unit_r(dx, flip=0):
        return ((x + dx) % NX) * 2 + (h + flip) % 2

    def unit_l(dz, flip=0):
        return ((z + dz) % NZ) * 2 + (l + flip) % 2

    def to_row(r):
        return (r, col)

    def to_col(c):
        return (row, c)

    x_up, x_down, y_far = to_row(unit_r(1)), to_row(unit_r(-1)), to_row(unit_r(0, 1))
    z_up, z_down = to_col(unit_l(1) * 2 + k), to_col(unit_l(-1) * 2 + k)
    y_near, sibling = to_col(unit_l(0, 1) * 2 + k), to_col((col // 2) * 2 + (1 - k))

    r_here = pltpu.make_async_copy(right, rbuf.at[row], cs.at[0])
    l_here = pltpu.make_async_copy(left, lbuf.at[col // 2, :, pl.ds(k * half, half), :], cs.at[1])
    s_here = pltpu.make_async_copy(slab, out, cs.at[2])
    small = [
        pltpu.make_async_copy(src, dst, cs.at[3 + i])
        for i, (src, dst) in enumerate([(est_in, est), (obs_in, obs), (arc_in, arc), (bias_in, bias)])
    ]
    for c in [r_here, *small, l_here, s_here]:
        c.start()

    barrier = pltpu.get_barrier_semaphore()
    for d in range(1, 16):
        pl.semaphore_signal(barrier, inc=1, device_id=to_col((col + d) % 16), device_id_type=MESH)
    for d in range(1, 8):
        pl.semaphore_signal(barrier, inc=1, device_id=to_row((row + d) % 8), device_id_type=MESH)
    r_here.wait()
    for c in small:
        c.wait()
    e = jnp.broadcast_to(est[...], (8, width))
    psend[...] = jnp.zeros_like(psend)
    for g in range(groups):
        p = lax.dot_general(
            e, rbuf[row, g], (((1,), (1,)), ((), ())),
            precision=lax.Precision.HIGHEST, preferred_element_type=F32,
        )
        psend[g : g + 1, :] = p[0:1, :]
    pl.semaphore_wait(barrier, 22)

    sends = []

    def remote(src, dst, s, r, target):
        return pltpu.make_async_remote_copy(
            src_ref=src, dst_ref=dst, send_sem=s, recv_sem=r, device_id=target, device_id_type=MESH
        )

    def r_copy(slot, unit, part, i, target, src=None):
        rows, cols = pl.ds(part * half, half), pl.ds(*CHUNKS[i])
        dst = rbuf.at[unit, :, rows, cols]
        s = slot * len(CHUNKS) + i
        return remote(dst if src is None else src.at[:, rows, cols], dst, rs.at[s], rr.at[s], target)

    def r_send(slot, unit, part, i, target, src=None):
        c = r_copy(slot, unit, part, i, target, src)
        c.start()
        sends.append(c)

    def r_wait(slot, unit, part, i):
        r_copy(slot, unit, part, i, y_far).wait_recv()

    def r_all(slot, unit, part):
        for i in range(len(CHUNKS)):
            r_wait(slot, unit, part, i)

    def l_rows(part, core):
        if part == "a":
            return pl.ds(core * half, quarter)
        if part == "b":
            return pl.ds(core * half + quarter, quarter)
        return pl.ds(core * half, half)

    def l_copy(slot, unit, part, target, src=None, core=None):
        dst = lbuf.at[unit, :, l_rows(part, k if core is None else core), :]
        if src is not None:
            src = src.at[:, l_rows(part, 0), :]
        return remote(dst if src is None else src, dst, ls.at[slot], lr.at[slot], target)

    def l_send(slot, unit, part, target, src=None):
        c = l_copy(slot, unit, part, target, src)
        c.start()
        sends.append(c)
        return c

    def l_wait(slot, unit, part, core=None):
        l_copy(slot, unit, part, sibling, core=core).wait_recv()

    own_r, own_l = row, col // 2
    for d in range(1, 16):
        c = remote(psend, pbuf.at[col], ps.at[d], pr.at[d], to_col((col + d) % 16))
        c.start()
        sends.append(c)
    near = l_send(0, own_l, "", y_near, left)
    for i in range(len(CHUNKS)):
        r_send(0, own_r, A, i, x_up, right)
        r_send(3, own_r, B, i, x_down, right)
    l_send(1, own_l, "a", z_up, left)
    l_send(4, own_l, "b", z_down, left)
    l_send(2, own_l, "b", z_up, left)
    l_send(3, own_l, "a", z_down, left)
    for i in range(len(CHUNKS)):
        r_send(1, own_r, B, i, x_up, right)
        r_send(2, own_r, A, i, x_down, right)
    l_send(13, own_l, "", sibling, left)
    def prepare(unit):
        def body(i, carry):
            cols = pl.ds(pl.multiple_of(i * TILE, TILE), TILE)
            for g in range(groups):
                t = lbuf[unit, g, :, cols].T * wbuf[unit, g : g + 1, :]
                hi = t.astype(BF16)
                lo = (t - hi.astype(F32)).astype(BF16)
                lt[unit, cols, g * n_obs : (g + 1) * n_obs] = hi
                lt[unit, cols, (groups + g) * n_obs : (groups + g + 1) * n_obs] = lo
            return carry

        lax.fori_loop(0, width // TILE, body, 0)

    depth = groups * n_obs

    def multiply_part(unit, i):
        cols = pl.ds(pl.multiple_of(i * TILE, TILE), TILE)
        t = rbuf[unit, :, :, cols].reshape(depth, TILE)
        hi = t.astype(BF16)
        lo = (t - hi.astype(F32)).astype(BF16)
        both = jnp.concatenate([hi, hi], axis=0)
        out[:, cols] += jnp.dot(lt[unit], both, preferred_element_type=F32) + jnp.dot(
            lt[unit, :, 0:depth], lo, preferred_element_type=F32
        )

    def multiply(*units):
        def body(i, carry):
            for unit in units:
                multiply_part(unit, i)
            return carry

        lax.fori_loop(0, width // TILE, body, 0)

    def first(i):
        r_wait(0, unit_r(-1), A, i)
        if i not in ALONG_X:
            r_send(8, unit_r(-1), A, i, y_far)
        r_send(6, unit_r(-1), A, i, x_up)
        r_wait(3, unit_r(1), B, i)
        if i not in ALONG_X:
            r_send(9, unit_r(1), B, i, y_far)
        r_send(7, unit_r(1), B, i, x_down)

    def second(i):
        r_wait(4, unit_r(0, 1), A, i)
        if i in ALONG_X:
            r_send(8, unit_r(0, 1), A, i, x_up)
        r_send(10, unit_r(0, 1), A, i, x_down)
        r_wait(5, unit_r(0, 1), B, i)
        if i in ALONG_X:
            r_send(9, unit_r(0, 1), B, i, x_down)
        r_send(11, unit_r(0, 1), B, i, x_up)

    def third(i):
        r_wait(8, unit_r(-1, 1), A, i)
        r_send(12, unit_r(-1, 1), A, i, x_up)
        r_wait(9, unit_r(1, 1), B, i)
        r_send(13, unit_r(1, 1), B, i, x_down)

    near.wait_send()
    sends[:] = [c for c in sends if c is not near]
    for i in range(len(CHUNKS)):
        r_send(4, own_r, A, i, y_far, right)
        r_send(5, own_r, B, i, y_far, right)
    l_wait(0, unit_l(0, 1), "")
    l_send(7, unit_l(0, 1), "a", z_up)
    l_send(10, unit_l(0, 1), "b", z_down)
    l_send(8, unit_l(0, 1), "b", z_up)
    l_send(9, unit_l(0, 1), "a", z_down)
    l_send(14, unit_l(0, 1), "", sibling)
    l_wait(1, unit_l(-1), "a")
    l_send(5, unit_l(-1), "a", z_up)
    l_wait(4, unit_l(1), "b")
    l_send(6, unit_l(1), "b", z_down)
    l_wait(2, unit_l(-1), "b")
    l_send(15, unit_l(-1), "", sibling)
    l_wait(3, unit_l(1), "a")
    l_send(16, unit_l(1), "", sibling)
    offset = jnp.zeros((groups, n_obs), F32)
    ids = arc[...]
    for a in range(bias.shape[0]):
        offset = jnp.where(ids == a, bias[a], offset)
    pbuf[col] = psend[...]
    for d in range(1, 16):
        remote(psend, pbuf.at[(col + 16 - d) % 16], ps.at[d], pr.at[d], sibling).wait_recv()
    total = pbuf[0]
    for c in range(1, 16):
        total = total + pbuf[c]
    residual = obs[...] - total[:groups] - offset
    wbuf[row] = jnp.zeros_like(wbuf[0])
    wbuf[row, 0:groups, :] = 1.0 / (1.0 + residual * residual)
    for d in range(1, 8):
        c = remote(wbuf.at[row], wbuf.at[row], ws.at[d], wr.at[d], to_row((row + d) % 8))
        c.start()
        sends.append(c)
    for i in range(len(CHUNKS)):
        first(i)
    for d in range(1, 8):
        u = (row + 8 - d) % 8
        remote(wbuf.at[row], wbuf.at[u], ws.at[d], wr.at[d], y_far).wait_recv()
    l_here.wait()
    l_wait(13, own_l, "", 1 - k)
    prepare(own_l)
    l_wait(14, unit_l(0, 1), "", 1 - k)
    prepare(unit_l(0, 1))
    l_wait(5, unit_l(2), "a")
    l_wait(6, unit_l(2), "b")
    l_send(17, unit_l(2), "", sibling)
    l_wait(15, unit_l(-1), "", 1 - k)
    prepare(unit_l(-1))
    l_wait(7, unit_l(-1, 1), "a")
    l_send(11, unit_l(-1, 1), "a", z_up)
    l_wait(10, unit_l(1, 1), "b")
    l_send(12, unit_l(1, 1), "b", z_down)
    l_wait(16, unit_l(1), "", 1 - k)
    prepare(unit_l(1))
    l_wait(8, unit_l(-1, 1), "b")
    l_send(18, unit_l(-1, 1), "", sibling)
    l_wait(9, unit_l(1, 1), "a")
    l_send(19, unit_l(1, 1), "", sibling)
    second(0)
    second(1)
    l_wait(17, unit_l(2), "", 1 - k)
    prepare(unit_l(2))
    l_wait(18, unit_l(-1, 1), "", 1 - k)
    prepare(unit_l(-1, 1))
    l_wait(19, unit_l(1, 1), "", 1 - k)
    prepare(unit_l(1, 1))
    second(2)
    s_here.wait()
    last = unit_l(2, 1)

    def early(unit):
        pl.when(unit != last)(lambda: multiply(unit))

    def late(unit):
        pl.when(unit == last)(lambda: multiply(unit))

    early(own_r)
    second(3)
    second(4)
    l_wait(11, unit_l(2, 1), "a")
    l_wait(12, unit_l(2, 1), "b")
    l_send(20, unit_l(2, 1), "", sibling)
    r_all(1, unit_r(-1), B)
    early(unit_r(-1))
    third(0)
    r_all(2, unit_r(1), A)
    early(unit_r(1))
    l_wait(20, unit_l(2, 1), "", 1 - k)
    prepare(last)
    late(own_r)
    late(unit_r(-1))
    late(unit_r(1))
    third(1)
    multiply(unit_r(0, 1))
    third(4)
    r_all(6, unit_r(2), A)
    r_all(7, unit_r(2), B)
    multiply(unit_r(2))
    for t, chunks in enumerate(OF_TILE):
        if t >= 2:
            third(t)
        for i in chunks:
            r_wait(10, unit_r(1, 1), A, i)
            r_wait(11, unit_r(-1, 1), B, i)
        multiply_part(unit_r(1, 1), t)
        multiply_part(unit_r(-1, 1), t)
    for t, chunks in enumerate(OF_TILE):
        for i in chunks:
            r_wait(12, unit_r(2, 1), A, i)
            r_wait(13, unit_r(2, 1), B, i)
        multiply_part(unit_r(2, 1), t)
    for c in sends:
        c.wait_send()


def local(normal_slab, left_design, right_design, estimate, observed, arc_id, arc_bias):
    groups, n_obs, width = right_design.shape
    rows = left_design.shape[2]
    dma = pltpu.SemaphoreType.DMA
    return pl.pallas_call(
        kernel,
        name="gather_and_update",
        out_shape=pltpu.VMEM(normal_slab.shape, F32),
        in_specs=[pl.BlockSpec(memory_space=pltpu.HBM)] * 7,
        out_specs=pl.BlockSpec(memory_space=pltpu.VMEM),
        scratch_shapes=[
            pltpu.VMEM((8, groups, n_obs, width), F32),
            pltpu.VMEM((8, groups, n_obs, rows), F32),
            pltpu.VMEM((8, rows, 2 * groups * n_obs), BF16),
            pltpu.VMEM((8, n_obs), F32),
            pltpu.VMEM((16, 8, n_obs), F32),
            pltpu.VMEM((8, 8, n_obs), F32),
            pltpu.VMEM((1, width), F32),
            pltpu.VMEM((groups, n_obs), F32),
            pltpu.VMEM((groups, n_obs), jnp.int32),
            pltpu.SMEM(arc_bias.shape, F32),
            dma((14 * len(CHUNKS),)), dma((14 * len(CHUNKS),)), dma((21,)), dma((21,)),
            dma((16,)), dma((16,)), dma((8,)), dma((8,)), dma((7,)),
        ],
        compiler_params=pltpu.CompilerParams(
            collective_id=0, has_side_effects=True, vmem_limit_bytes=59 * 1024 * 1024
        ),
    )(estimate[None, :], observed, arc_id, arc_bias, normal_slab, left_design, right_design)


def solution(mesh):
    in_specs = (
        P("row", "col"),
        P(None, "col", "row"),
        P(None, "row", "col"),
        P("col"),
        P(None, "row"),
        P(None, "row"),
        P(),
    )
    return jax.shard_map(local, mesh=mesh, in_specs=in_specs, out_specs=P("row", "col"), check_vma=False)
```

time: 116 us -> 112 us (0.966)
  Pallas kernels: 114 us -> 110 us
    pallas_call x1, Pallas kernels: 114 us -> 110 us  [local(): pl.pallas_call(kernel, name='gather_and_update', out_shape=pltpu.VMEM(nor...]
where the time goes in v3:
time: 112 us
  Pallas kernels  110 us (98%)
  local copies, waits for them, and re-layouts  2.02 us (2%)
    pallas_call x1, Pallas kernels, local(): pl.pallas_call(kernel, name='gather_and_update', out_shape=pltpu.VMEM(nor...  110 us

profile of v3, /device:TPU:0, one launch (start us, length us, event | category | flops | bytes accessed | tf_op | source)
XLA Modules:
  0.0 111.7 jit_solution(3728854539298910641)
XLA Ops:
  0.0 109.7 %gather_and_update.1 = f32[1024,1024]{1,0:T(8,128)S(1)} custom-call(f32[1,1024]{1,0:T(1,128)} %bitcast.1, f32[3,128]{1,0:T(4,128)} %obs_in.1, s32[3,128]{1,0:T(4,128)} %arc_in.1, f32[64]{0:T(128)} %bias_in.1, f32[1024,1024]{1,0:T(8,128)} %slab.1, f32[3,64,1024]{2,1,0:T(8,128)} %left.1, f32[3,128,1024]{2,1,0:T(8,128)} %right.1), custom_call_target="tpu_custom_call" | custom-call | tf_op jit(solution)/shard_map/gather_and_update/pallas_call | solution.py:317
  109.7 2.0 %copy.9 = f32[1024,1024]{1,0:T(8,128)} copy(f32[1024,1024]{1,0:T(8,128)S(1)} %gather_and_update.1) | data formatting | bytes 8388608

commit v4 on v3

--- a/solution.py
+++ b/solution.py
@@ -129,9 +129,6 @@
     l_send(4, own_l, "b", z_down, left)
     l_send(2, own_l, "b", z_up, left)
     l_send(3, own_l, "a", z_down, left)
-    for i in range(len(CHUNKS)):
-        r_send(1, own_r, B, i, x_up, right)
-        r_send(2, own_r, A, i, x_down, right)
     l_send(13, own_l, "", sibling, left)
     def prepare(unit):
         def body(i, carry):
@@ -168,12 +165,8 @@
 
     def first(i):
         r_wait(0, unit_r(-1), A, i)
-        if i not in ALONG_X:
-            r_send(8, unit_r(-1), A, i, y_far)
         r_send(6, unit_r(-1), A, i, x_up)
         r_wait(3, unit_r(1), B, i)
-        if i not in ALONG_X:
-            r_send(9, unit_r(1), B, i, y_far)
         r_send(7, unit_r(1), B, i, x_down)
 
     def second(i):
@@ -186,15 +179,24 @@
             r_send(9, unit_r(0, 1), B, i, x_down)
         r_send(11, unit_r(0, 1), B, i, x_up)
 
+    def cross(i):
+        r_send(8, unit_r(-1), A, i, y_far)
+        r_send(9, unit_r(1), B, i, y_far)
+
     def third(i):
         r_wait(8, unit_r(-1, 1), A, i)
         r_send(12, unit_r(-1, 1), A, i, x_up)
         r_wait(9, unit_r(1, 1), B, i)
         r_send(13, unit_r(1, 1), B, i, x_down)
 
+    for i in range(2):
+        first(i)
+    for i in range(len(CHUNKS)):
+        r_send(1, own_r, B, i, x_up, right)
+        r_send(2, own_r, A, i, x_down, right)
     near.wait_send()
     sends[:] = [c for c in sends if c is not near]
-    for i in range(len(CHUNKS)):
+    for i in range(2):
         r_send(4, own_r, A, i, y_far, right)
         r_send(5, own_r, B, i, y_far, right)
     l_wait(0, unit_l(0, 1), "")
@@ -228,8 +230,11 @@
         c = remote(wbuf.at[row], wbuf.at[row], ws.at[d], wr.at[d], to_row((row + d) % 8))
         c.start()
         sends.append(c)
-    for i in range(len(CHUNKS)):
+    for i in range(2, len(CHUNKS)):
         first(i)
+    for i in range(2, len(CHUNKS)):
+        r_send(4, own_r, A, i, y_far, right)
+        r_send(5, own_r, B, i, y_far, right)
     for d in range(1, 8):
         u = (row + 8 - d) % 8
         remote(wbuf.at[row], wbuf.at[u], ws.at[d], wr.at[d], y_far).wait_recv()
@@ -255,6 +260,7 @@
     l_send(19, unit_l(1, 1), "", sibling)
     second(0)
     second(1)
+    cross(0)
     l_wait(17, unit_l(2), "", 1 - k)
     prepare(unit_l(2))
     l_wait(18, unit_l(-1, 1), "", 1 - k)
@@ -262,6 +268,7 @@
     l_wait(19, unit_l(1, 1), "", 1 - k)
     prepare(unit_l(1, 1))
     second(2)
+    cross(1)
     s_here.wait()
     last = unit_l(2, 1)
 
@@ -273,26 +280,30 @@
 
     early(own_r)
     second(3)
+    cross(2)
     second(4)
+    cross(3)
     l_wait(11, unit_l(2, 1), "a")
     l_wait(12, unit_l(2, 1), "b")
     l_send(20, unit_l(2, 1), "", sibling)
     r_all(1, unit_r(-1), B)
     early(unit_r(-1))
-    third(0)
     r_all(2, unit_r(1), A)
     early(unit_r(1))
+    early(unit_r(0, 1))
+    third(0)
+    r_all(6, unit_r(2), A)
+    r_all(7, unit_r(2), B)
+    early(unit_r(2))
+    third(1)
+    third(4)
     l_wait(20, unit_l(2, 1), "", 1 - k)
     prepare(last)
     late(own_r)
     late(unit_r(-1))
     late(unit_r(1))
-    third(1)
-    multiply(unit_r(0, 1))
-    third(4)
-    r_all(6, unit_r(2), A)
-    r_all(7, unit_r(2), B)
-    multiply(unit_r(2))
+    late(unit_r(0, 1))
+    late(unit_r(2))
     for t, chunks in enumerate(OF_TILE):
         if t >= 2:
             third(t)

time: 112 us -> 105 us (0.938)
  Pallas kernels: 110 us -> 102 us
    pallas_call x1, Pallas kernels: 110 us -> 102 us  [local(): pl.pallas_call(kernel, name='gather_and_update', out_shape=pltpu.VMEM(nor...]
where the time goes in v4:
time: 105 us; the launch traced here: 104 us
  Pallas kernels  102 us (97%)
  local copies, waits for them, and re-layouts  2.02 us (2%)
    pallas_call x1, Pallas kernels, local(): pl.pallas_call(kernel, name='gather_and_update', out_shape=pltpu.VMEM(nor...  102 us

profile of v4, /device:TPU:0, one launch (start us, length us, event | category | flops | bytes accessed | tf_op | source)
XLA Modules:
  0.0 103.7 jit_solution(16335159486475316873)
XLA Ops:
  0.0 101.7 %gather_and_update.1 = f32[1024,1024]{1,0:T(8,128)S(1)} custom-call(f32[1,1024]{1,0:T(1,128)} %bitcast.1, f32[3,128]{1,0:T(4,128)} %obs_in.1, s32[3,128]{1,0:T(4,128)} %arc_in.1, f32[64]{0:T(128)} %bias_in.1, f32[1024,1024]{1,0:T(8,128)} %slab.1, f32[3,64,1024]{2,1,0:T(8,128)} %left.1, f32[3,128,1024]{2,1,0:T(8,128)} %right.1), custom_call_target="tpu_custom_call" | custom-call | tf_op jit(solution)/shard_map/gather_and_update/pallas_call | solution.py:328
  101.7 2.0 %copy.9 = f32[1024,1024]{1,0:T(8,128)} copy(f32[1024,1024]{1,0:T(8,128)S(1)} %gather_and_update.1) | data formatting | bytes 8388608

commit v5 on v4

--- a/solution.py
+++ b/solution.py
@@ -267,36 +267,34 @@
     prepare(unit_l(-1, 1))
     l_wait(19, unit_l(1, 1), "", 1 - k)
     prepare(unit_l(1, 1))
+    s_here.wait()
+    last = unit_l(2, 1)
+
+    def early(unit):
+        pl.when(unit != last)(lambda: multiply(unit))
+
+    def late(unit):
+        pl.when(unit == last)(lambda: multiply(unit))
+
+    early(own_r)
     second(2)
     cross(1)
-    s_here.wait()
-    last = unit_l(2, 1)
-
-    def early(unit):
-        pl.when(unit != last)(lambda: multiply(unit))
-
-    def late(unit):
-        pl.when(unit == last)(lambda: multiply(unit))
-
-    early(own_r)
+    r_all(1, unit_r(-1), B)
+    early(unit_r(-1))
     second(3)
     cross(2)
     second(4)
     cross(3)
+    r_all(2, unit_r(1), A)
+    early(unit_r(1))
     l_wait(11, unit_l(2, 1), "a")
     l_wait(12, unit_l(2, 1), "b")
     l_send(20, unit_l(2, 1), "", sibling)
-    r_all(1, unit_r(-1), B)
-    early(unit_r(-1))
-    r_all(2, unit_r(1), A)
-    early(unit_r(1))
     early(unit_r(0, 1))
     third(0)
     r_all(6, unit_r(2), A)
     r_all(7, unit_r(2), B)
     early(unit_r(2))
-    third(1)
-    third(4)
     l_wait(20, unit_l(2, 1), "", 1 - k)
     prepare(last)
     late(own_r)
@@ -304,19 +302,31 @@
     late(unit_r(1))
     late(unit_r(0, 1))
     late(unit_r(2))
-    for t, chunks in enumerate(OF_TILE):
-        if t >= 2:
-            third(t)
-        for i in chunks:
+    third(1)
+    third(4)
+    def pair(t):
+        for i in OF_TILE[t]:
             r_wait(10, unit_r(1, 1), A, i)
             r_wait(11, unit_r(-1, 1), B, i)
         multiply_part(unit_r(1, 1), t)
         multiply_part(unit_r(-1, 1), t)
-    for t, chunks in enumerate(OF_TILE):
-        for i in chunks:
+
+    def final(t):
+        for i in OF_TILE[t]:
             r_wait(12, unit_r(2, 1), A, i)
             r_wait(13, unit_r(2, 1), B, i)
         multiply_part(unit_r(2, 1), t)
+
+    pair(0)
+    pair(1)
+    final(0)
+    third(2)
+    pair(2)
+    final(1)
+    third(3)
+    pair(3)
+    final(2)
+    final(3)
     for c in sends:
         c.wait_send()
 

time: 105 us -> 103 us (0.981); the launches traced: 104 us -> 103 us
  no operation moved by 1% of the time
where the time goes in v5:
time: 103 us
  Pallas kernels  101 us (98%)
  local copies, waits for them, and re-layouts  2.02 us (2%)
    pallas_call x1, Pallas kernels, local(): pl.pallas_call(kernel, name='gather_and_update', out_shape=pltpu.VMEM(nor...  101 us

profile of v5, /device:TPU:0, one launch (start us, length us, event | category | flops | bytes accessed | tf_op | source)
XLA Modules:
  0.0 102.9 jit_solution(7878791184496204672)
XLA Ops:
  0.0 100.8 %gather_and_update.1 = f32[1024,1024]{1,0:T(8,128)S(1)} custom-call(f32[1,1024]{1,0:T(1,128)} %bitcast.1, f32[3,128]{1,0:T(4,128)} %obs_in.1, s32[3,128]{1,0:T(4,128)} %arc_in.1, f32[64]{0:T(128)} %bias_in.1, f32[1024,1024]{1,0:T(8,128)} %slab.1, f32[3,64,1024]{2,1,0:T(8,128)} %left.1, f32[3,128,1024]{2,1,0:T(8,128)} %right.1), custom_call_target="tpu_custom_call" | custom-call | tf_op jit(solution)/shard_map/gather_and_update/pallas_call | solution.py:338
  100.9 2.0 %copy.9 = f32[1024,1024]{1,0:T(8,128)} copy(f32[1024,1024]{1,0:T(8,128)S(1)} %gather_and_update.1) | data formatting | bytes 8388608
